TPU v7x, 1024 devices: a whole 4x8x16 slice. The times are simulated.
1024 devices in a mesh: node: 32 (over y, z_hi), local: 32 (over x, z_lo, core).
Axes of the slice: x: 4, y: 8, z: 16 (z_hi: 4, z_lo: 4; z = z_hi * 4 + z_lo), core: 2. Of those that a mesh axis runs over, the one named last changes fastest.
Arguments:
- tok_x: bfloat16 [2048, 2048], P(('node', 'local')), may hold values from -6 to 6
- grad_out: bfloat16 [2048, 2048], P(('node', 'local')), may hold values from -6 to 6
- expert_ids: int32 [2048, 8], P('node'), may hold values from 0 to 127, as said below
- slot_ids: int32 [2048, 8], P('node'), may hold values from 0 to 63, as said below
- route_probs: bfloat16 [2048, 8], P('node'), may hold values from 0.099609375 to 1
- gate_weight: bfloat16 [1024, 96, 2048], P(('node', 'local')), may hold values from -0.125 to 0.125
- up_weight: bfloat16 [1024, 96, 2048], P(('node', 'local')), may hold values from -0.125 to 0.125
- down_weight: bfloat16 [1024, 96, 2048], P(('node', 'local')), may hold values from -0.21875 to 0.21875
Outputs:
- grad_x: bfloat16 [2048, 2048], P(('node', 'local'))
- grad_probs: float32 [2048, 8], P(('node', 'local'))
- grad_gate: float32 [1024, 96, 2048], P(('node', 'local'))
- grad_up: float32 [1024, 96, 2048], P(('node', 'local'))
- grad_down: float32 [1024, 96, 2048], P(('node', 'local'))
Inputs may be any that keep to these rules, and one draw needn't show every extreme that they name: `expert_ids`: each token names 8 different experts. Among the 64 tokens of every index of node, some expert is named by all 64 tokens. `slot_ids`: the pairs of the 64 tokens of one index of node that name one expert carry the slots 0, 1, 2 and so on, each once.
All inputs are finite; a program needn't handle non-finite values.
Results may differ from a plain program's by a relative error of at most 0.0049.
Values may be sent and summed in bfloat16 or wider, within the bound.
No kernel may reach another device: no remote copies, remote signals or barrier semaphores. Data moves between devices by JAX's collectives and lax.ppermute only.
A program may use at most 32 MiB of HBM per device.

v0:
```python
import jax
import jax.numpy as jnp
from jax import lax
from jax.sharding import PartitionSpec as P

EXP_NODE = 4
CAPN = 7


contract_last = (((1,), (1,)), ((), ()))
contract_first = (((0,), (0,)), ((), ()))


def owner_grads(owner_x, owner_d, owner_p, w_gate_rows, w_up_rows, w_down_rows):
    gate_pre = lax.dot_general(
        owner_x, w_gate_rows, contract_last, preferred_element_type=jnp.float32
    )
    up_pre = lax.dot_general(owner_x, w_up_rows, contract_last, preferred_element_type=jnp.float32)
    sigmoid_gate = jax.nn.sigmoid(gate_pre)
    activated = gate_pre * sigmoid_gate
    hidden = activated * up_pre
    back_proj = lax.dot_general(
        owner_d, w_down_rows, contract_last, preferred_element_type=jnp.float32
    )
    pair_grad = jnp.sum(hidden * back_proj, axis=1)
    d_hidden = owner_p[:, None] * back_proj
    d_gate = (d_hidden * up_pre * sigmoid_gate * (1.0 + gate_pre * (1.0 - sigmoid_gate))).astype(
        jnp.bfloat16
    )
    d_up = (d_hidden * activated).astype(jnp.bfloat16)
    scaled_hidden = (owner_p[:, None] * hidden).astype(jnp.bfloat16)
    input_grad = jnp.dot(d_gate, w_gate_rows, preferred_element_type=jnp.float32) + jnp.dot(
        d_up, w_up_rows, preferred_element_type=jnp.float32
    )
    gate_grad = lax.dot_general(d_gate, owner_x, contract_first, preferred_element_type=jnp.float32)
    up_grad = lax.dot_general(d_up, owner_x, contract_first, preferred_element_type=jnp.float32)
    down_grad = lax.dot_general(
        scaled_hidden, owner_d, contract_first, preferred_element_type=jnp.float32
    )
    return (input_grad, pair_grad, gate_grad, up_grad, down_grad)


def local(tok_x, grad_out, expert_ids, slot_ids, route_probs, gate_weight, up_weight, down_weight):
    node_count = lax.axis_size("node")
    owners = lax.axis_size("local") // EXP_NODE
    place = lax.axis_index("local")
    own_class = place // owners
    node_tokens = expert_ids.shape[0]
    top_count = expert_ids.shape[1]
    model_width = tok_x.shape[1]
    pair_count = node_tokens * top_count
    node_x, node_d = (
        lax.all_gather(tok_x, "local", axis=0, tiled=True),
        lax.all_gather(grad_out, "local", axis=0, tiled=True),
    )
    flat_expert = expert_ids.reshape(-1)
    flat_slot = slot_ids.reshape(-1)
    pair_ids = jnp.arange(pair_count, dtype=jnp.int32)
    is_mine = (flat_expert % EXP_NODE == own_class) & (flat_slot < CAPN)
    target = jnp.where(is_mine, flat_expert // EXP_NODE * CAPN + flat_slot, node_count * CAPN)
    slot_table = (
        jnp.full((node_count * CAPN,), pair_count, jnp.int32).at[target].set(pair_ids, mode="drop")
    )
    token_rows = slot_table // top_count
    outbox_p = jnp.take(route_probs.reshape(-1), slot_table, mode="fill", fill_value=0).reshape(
        node_count, CAPN
    )
    outbox_x = jnp.take(node_x, token_rows, axis=0, mode="fill", fill_value=0).reshape(
        node_count, CAPN, model_width
    )
    outbox_d = jnp.take(node_d, token_rows, axis=0, mode="fill", fill_value=0).reshape(
        node_count, CAPN, model_width
    )
    arrived_x, arrived_d, arrived_p = (
        lax.all_to_all(outbox_x, "node", split_axis=0, concat_axis=0, tiled=True),
        lax.all_to_all(outbox_d, "node", split_axis=0, concat_axis=0, tiled=True),
        lax.all_to_all(outbox_p, "node", split_axis=0, concat_axis=0, tiled=True),
    )
    owner_x = arrived_x.reshape(-1, model_width)
    owner_d = arrived_d.reshape(-1, model_width)
    owner_p = arrived_p.reshape(-1).astype(jnp.float32)
    input_grad, pair_grad, gate_grad, up_grad, down_grad = owner_grads(
        owner_x, owner_d, owner_p, gate_weight[0], up_weight[0], down_weight[0]
    )
    token_hits = (token_rows[None, :] == jnp.arange(node_tokens, dtype=jnp.int32)[:, None]).astype(
        jnp.float32
    )
    back_x, back_p = (
        lax.all_to_all(
            input_grad.reshape(node_count, CAPN, model_width),
            "node",
            split_axis=0,
            concat_axis=0,
            tiled=True,
        ),
        lax.all_to_all(
            pair_grad.reshape(node_count, CAPN), "node", split_axis=0, concat_axis=0, tiled=True
        ),
    )
    token_x = jnp.dot(
        token_hits,
        back_x.reshape(-1, model_width),
        precision=lax.Precision.HIGHEST,
        preferred_element_type=jnp.float32,
    )
    token_p = (
        jnp.zeros((pair_count,), jnp.float32)
        .at[slot_table]
        .add(back_p.reshape(-1), mode="drop")
        .reshape(node_tokens, top_count)
    )
    summed_x, summed_p = (
        lax.psum_scatter(token_x, "local", scatter_dimension=0, tiled=True),
        lax.psum_scatter(token_p, "local", scatter_dimension=0, tiled=True),
    )
    return (
        summed_x.astype(jnp.bfloat16),
        summed_p,
        gate_grad[None],
        up_grad[None],
        down_grad[None],
    )


def solution(mesh):
    in_specs = (
        P(("node", "local"), None),
        P(("node", "local"), None),
        P("node", None),
        P("node", None),
        P("node", None),
        P(("node", "local"), None, None),
        P(("node", "local"), None, None),
        P(("node", "local"), None, None),
    )
    out_specs = (
        P(("node", "local"), None),
        P(("node", "local"), None),
        P(("node", "local"), None, None),
        P(("node", "local"), None, None),
        P(("node", "local"), None, None),
    )
    return jax.shard_map(local, mesh=mesh, in_specs=in_specs, out_specs=out_specs, check_vma=False)
```

profile of v0, /device:TPU:1, one launch (start us, length us, event | category | flops | bytes accessed | tf_op | source)
XLA Modules:
  0.0 550.6 jit_solution(1543090887848090723)
XLA Ops:
  2.5 2.4 scatter_custom_fusion
  6.4 1.9 gather_fusion
  9.1 24.9 %all-to-all-start = ((bf16[32,1,7]{2,1,0:T(2,128)(2,1)}), bf16[32,1,7]{2,1,0:T(2,128)(2,1)S(1)}, u32[]{:S(2)}, u32[]{:S(2)}) async-start(bf16[32,1,7]{2,1,0:T(2,128)(2,1)} %select_n.97), calls=%async_computation | async-start | bytes 32768 | tf_op jit(solution)/shard_map/all_to_all | solution.py:77
  34.6 45.1 %all-gather.1 = bf16[32,2,2048]{2,1,0:T(2,128)(2,1)S(1)} all-gather(bf16[1,2,2048]{2,1,0:T(2,128)(2,1)} %bitcast.37), channel_id=1, replica_groups=mesh['node'=32,'local'=32] {'local'}, dimensions={0}, use_global_device_ids=true | all-gather | bytes 270336 | tf_op jit(solution)/shard_map/all_gather | solution.py:53
  79.8 39.2 %all-gather = bf16[32,2,2048]{2,1,0:T(2,128)(2,1)S(1)} all-gather(bf16[1,2,2048]{2,1,0:T(2,128)(2,1)} %bitcast.38), channel_id=1, replica_groups=mesh['node'=32,'local'=32] {'local'}, dimensions={0}, use_global_device_ids=true | all-gather | bytes 270336 | tf_op jit(solution)/shard_map/all_gather | solution.py:54
  124.0 16.7 %all-to-all-start.2 = ((bf16[32,7,2048]{2,1,0:T(8,128)(2,1)}), bf16[32,7,2048]{2,1,0:T(8,128)(2,1)S(1)}, u32[]{:S(2)}, u32[]{:S(2)}) async-start(bf16[32,7,2048]{2,1,0:T(8,128)(2,1)} %reshape.232), calls=%async_computation.2 | async-start | bytes 2097152 | tf_op jit(solution)/shard_map/all_to_all | solution.py:75
  142.0 54.8 %all-to-all-done.2 = bf16[32,7,2048]{2,1,0:T(8,128)(2,1)S(1)} async-done(((bf16[32,7,2048]{2,1,0:T(8,128)(2,1)}), bf16[32,7,2048]{2,1,0:T(8,128)(2,1)S(1)}, u32[]{:S(2)}, u32[]{:S(2)}) %all-to-all-start.2) | async-done | bytes 917536 | tf_op jit(solution)/shard_map/all_to_all | solution.py:75
  196.7 23.6 %all-to-all-start.1 = ((bf16[32,7,2048]{2,1,0:T(8,128)(2,1)}), bf16[32,7,2048]{2,1,0:T(8,128)(2,1)S(1)}, u32[]{:S(2)}, u32[]{:S(2)}) async-start(bf16[32,7,2048]{2,1,0:T(8,128)(2,1)} %reshape.230), calls=%async_computation.1 | async-start | bytes 2097152 | tf_op jit(solution)/shard_map/all_to_all | solution.py:76
  221.3 2.1 fusion.5
  223.4 34.4 %all-to-all-done.1 = bf16[32,7,2048]{2,1,0:T(8,128)(2,1)S(1)} async-done(((bf16[32,7,2048]{2,1,0:T(8,128)(2,1)}), bf16[32,7,2048]{2,1,0:T(8,128)(2,1)S(1)}, u32[]{:S(2)}, u32[]{:S(2)}) %all-to-all-start.1) | async-done | bytes 917536 | tf_op jit(solution)/shard_map/all_to_all | solution.py:76
  258.1 2.4 multiply_reduce_fusion
  262.3 8.6 %all-to-all-start.4 = ((f32[32,1,7]{2,1,0:T(1,128)}), f32[32,1,7]{2,1,0:T(1,128)}, u32[]{:S(2)}, u32[]{:S(2)}) async-start(f32[32,1,7]{2,1,0:T(1,128)} %bitcast.6), calls=%async_computation.4 | async-start | bytes 32768 | tf_op jit(solution)/shard_map/all_to_all | solution.py:96
  270.9 2.4 convolution_add_fusion
  273.3 2.9 reshape.234
  276.2 61.4 %all-to-all-done.4 = f32[32,1,7]{2,1,0:T(1,128)} async-done(((f32[32,1,7]{2,1,0:T(1,128)}), f32[32,1,7]{2,1,0:T(1,128)}, u32[]{:S(2)}, u32[]{:S(2)}) %all-to-all-start.4) | async-done | bytes 928 | tf_op jit(solution)/shard_map/all_to_all | solution.py:96
  337.6 6.8 %all-to-all-start.3 = ((f32[32,7,2048]{2,1,0:T(8,128)}), f32[32,7,2048]{2,1,0:T(8,128)S(1)}, u32[]{:S(2)}, u32[]{:S(2)}) async-start(f32[32,7,2048]{2,1,0:T(8,128)} %reshape.234), calls=%async_computation.3 | async-start | bytes 4194304 | tf_op jit(solution)/shard_map/all_to_all | solution.py:89
  344.4 1.3 dynamic-slice
  347.5 2.0 convolution_bitcast_fusion.2
  351.2 1.3 reduce.7
  352.6 2.2 scatter_custom_fusion.1
  354.9 53.4 %all-to-all-done.3 = f32[32,7,2048]{2,1,0:T(8,128)S(1)} async-done(((f32[32,7,2048]{2,1,0:T(8,128)}), f32[32,7,2048]{2,1,0:T(8,128)S(1)}, u32[]{:S(2)}, u32[]{:S(2)}) %all-to-all-start.3) | async-done | bytes 1835040 | tf_op jit(solution)/shard_map/all_to_all | solution.py:89
  408.4 1.5 reshape.235
  409.9 2.3 fusion.10
  412.2 137.2 %all-reduce.4 = (bf16[64,2048]{1,0:T(8,128)(2,1)S(1)}, f32[64,8]{1,0:T(8,128)S(1)}) all-reduce(f32[64,2048]{1,0:T(8,128)S(1)} %fusion.10, f32[64,8]{1,0:T(8,128)S(1)} %reshape.237), channel_id=2, replica_groups=mesh['node'=32,'local'=32] {'local'}, use_global_device_ids=true, to_apply=%region_1.3.clone | all-reduce | flops 131584 | bytes 790528
  (67 shorter events, 18.1 us)
Async XLA Ops:
  0.6 220.2 %copy-start = (bf16[1,96,2048]{2,1,0:T(8,128)(2,1)S(1)}, bf16[1,96,2048]{2,1,0:T(8,128)(2,1)}, u32[]{:S(2)}) copy-start(bf16[1,96,2048]{2,1,0:T(8,128)(2,1)} %param.15) | copy-start | bytes 1179652
  4.9 0.6 copy-start.14
  9.1 114.9 %all-to-all-start = ((bf16[32,1,7]{2,1,0:T(2,128)(2,1)}), bf16[32,1,7]{2,1,0:T(2,128)(2,1)S(1)}, u32[]{:S(2)}, u32[]{:S(2)}) async-start(bf16[32,1,7]{2,1,0:T(2,128)(2,1)} %select_n.97), calls=%async_computation | async-start | bytes 32768 | tf_op jit(solution)/shard_map/all_to_all | solution.py:77
  34.0 0.6 copy-start.10
  122.7 18.0 %copy-start.3 = (bf16[224,2048]{1,0:T(8,128)(2,1)S(1)}, bf16[224,2048]{1,0:T(8,128)(2,1)}, u32[]{:S(2)}) copy-start(bf16[224,2048]{1,0:T(8,128)(2,1)} %get-tuple-element.13) | copy-start | bytes 2752516
  124.0 72.8 %all-to-all-start.2 = ((bf16[32,7,2048]{2,1,0:T(8,128)(2,1)}), bf16[32,7,2048]{2,1,0:T(8,128)(2,1)S(1)}, u32[]{:S(2)}, u32[]{:S(2)}) async-start(bf16[32,7,2048]{2,1,0:T(8,128)(2,1)} %reshape.232), calls=%async_computation.2 | async-start | bytes 2097152 | tf_op jit(solution)/shard_map/all_to_all | solution.py:75
  196.7 61.0 %all-to-all-start.1 = ((bf16[32,7,2048]{2,1,0:T(8,128)(2,1)}), bf16[32,7,2048]{2,1,0:T(8,128)(2,1)S(1)}, u32[]{:S(2)}, u32[]{:S(2)}) async-start(bf16[32,7,2048]{2,1,0:T(8,128)(2,1)} %reshape.230), calls=%async_computation.1 | async-start | bytes 2097152 | tf_op jit(solution)/shard_map/all_to_all | solution.py:76
  220.5 37.6 %copy-start.12 = (f32[224]{0:T(256)}, f32[224]{0:T(256)S(1)}, u32[]{:S(2)}) copy-start(f32[224]{0:T(256)S(1)} %reshape.238) | copy-start | bytes 2692
  221.3 39.2 %copy-start.5 = (f32[224,96]{0,1:T(8,128)}, f32[224,96]{0,1:T(8,128)S(1)}, u32[]{:S(2)}) copy-start(f32[224,96]{0,1:T(8,128)S(1)} %fusion.2) | copy-start | bytes 258052
  258.1 2.4 copy-start.1
  258.1 12.8 %copy-start.4 = (bf16[1,96,2048]{2,1,0:T(8,128)(2,1)S(1)}, bf16[1,96,2048]{2,1,0:T(8,128)(2,1)}, u32[]{:S(2)}) copy-start(bf16[1,96,2048]{2,1,0:T(8,128)(2,1)} %param.16) | copy-start | bytes 1179652
  260.5 0.6 copy-start.9
  262.3 75.3 %all-to-all-start.4 = ((f32[32,1,7]{2,1,0:T(1,128)}), f32[32,1,7]{2,1,0:T(1,128)}, u32[]{:S(2)}, u32[]{:S(2)}) async-start(f32[32,1,7]{2,1,0:T(1,128)} %bitcast.6), calls=%async_computation.4 | async-start | bytes 32768 | tf_op jit(solution)/shard_map/all_to_all | solution.py:96
  276.2 70.1 %copy-start.8 = (bf16[224,96]{0,1:T(8,128)(2,1)S(1)}, bf16[224,96]{0,1:T(8,128)(2,1)}, u32[]{:S(2)}) copy-start(bf16[224,96]{0,1:T(8,128)(2,1)} %get-tuple-element.12) | copy-start | bytes 129028
  337.6 70.8 %all-to-all-start.3 = ((f32[32,7,2048]{2,1,0:T(8,128)}), f32[32,7,2048]{2,1,0:T(8,128)S(1)}, u32[]{:S(2)}, u32[]{:S(2)}) async-start(f32[32,7,2048]{2,1,0:T(8,128)} %reshape.234), calls=%async_computation.3 | async-start | bytes 4194304 | tf_op jit(solution)/shard_map/all_to_all | solution.py:89
  344.3 5.2 copy-start.6
  346.3 3.2 copy-start.2
  346.3 3.2 copy-start.7
  346.3 3.2 copy-start.13
  354.9 55.0 %copy-start.11 = (s32[224]{0:T(256)S(1)}, s32[224]{0:T(256)}, u32[]{:S(2)}) copy-start(s32[224]{0:T(256)} %copy-done.10) | copy-start | bytes 2692
where the time goes:
time: 560 us; the launch traced here: 551 us
  blocking collectives  221 us (39%)
  waiting for transfers between devices  204 us (36%)
  starting transfers between devices  80.6 us (14%)
  local copies, waits for them, and re-layouts  23.7 us (4%)
  matrix products  14.4 us (3%)
    unnamed x1, blocking collectives  137 us
    all_to_all x1, waiting for transfers between devices, local(): lax.all_to_all(pair_grad.reshape(node_count, CAPN), 'node', split_axis=0,...  61.4 us
    all_to_all x1, waiting for transfers between devices, local(): lax.all_to_all(outbox_x, 'node', split_axis=0, concat_axis=0, tiled=True)  54.8 us
    all_to_all x1, waiting for transfers between devices, local(): lax.all_to_all(input_grad.reshape(node_count, CAPN, model_width), 'node',...  53.4 us
    all_gather x1, blocking collectives, local(): lax.all_gather(tok_x, 'local', axis=0, tiled=True)  45.1 us
    all_gather x1, blocking collectives, local(): lax.all_gather(grad_out, 'local', axis=0, tiled=True)  39.2 us
    all_to_all x1, waiting for transfers between devices, local(): lax.all_to_all(outbox_d, 'node', split_axis=0, concat_axis=0, tiled=True)  34.4 us
    all_to_all x1, starting transfers between devices, local(): lax.all_to_all(outbox_p, 'node', split_axis=0, concat_axis=0, tiled=True)  24.9 us
  transfers between devices with their start and end apart: 5, of which 4 were waited for; matrix products, arithmetic and copies ran while one was open for 4% of the time, Pallas kernels for 0%

commit v1 on v0

v1 whole, which is shorter than its diff:
```python
import jax
import jax.numpy as jnp
from jax import lax
from jax.experimental import pallas as pl
from jax.experimental.pallas import tpu as pltpu
from jax.sharding import PartitionSpec as P

NODES = 32
CLASSES = 4
ZL = 4
CORES = 2
COLS = ZL * CORES
CAPN = 7
SLOTS = 8
ROWS = NODES * SLOTS
TOPK = 8
TOK = 64
D = 2048
CB = D // COLS
HID = 96
LANES = 128
BF = jnp.bfloat16
F32 = jnp.float32

NT = (((1,), (1,)), ((), ()))
NN = (((1,), (0,)), ((), ()))
TN = (((0,), (0,)), ((), ()))


def dot(a, b, dims):
    return lax.dot_general(a, b, dims, preferred_element_type=F32)


def shift_pairs(step):
    return [
        (x * COLS + z * CORES + c, x * COLS + ((z + step) % ZL) * CORES + c)
        for x in range(CLASSES)
        for z in range(ZL)
        for c in range(CORES)
    ]


CORE_PAIRS = [(i, i ^ 1) for i in range(CLASSES * COLS)]


def targets(ids, slots, own_class):
    keep = ((ids & (CLASSES - 1)) == own_class) & (slots < CAPN)
    return jnp.where(keep, (ids >> 2) * SLOTS + slots, -1)


def row_iotas():
    lane = lax.broadcasted_iota(jnp.int32, (ROWS, LANES), 1)
    sub = lax.broadcasted_iota(jnp.int32, (ROWS, LANES), 0) & (SLOTS - 1)
    return lane, sub


def spread_column(column):
    lane, sub = row_iotas()
    put = jnp.where(lane == sub, column, 0.0).reshape(NODES, SLOTS, LANES)
    group = jnp.sum(put, axis=1, keepdims=True)
    return jnp.broadcast_to(group, (NODES, SLOTS, LANES)).reshape(ROWS, LANES)


def gather_column(block):
    lane, sub = row_iotas()
    last = block.reshape(NODES, SLOTS, LANES)[:, SLOTS - 1 :, :]
    last = jnp.broadcast_to(last, (NODES, SLOTS, LANES)).reshape(ROWS, LANES)
    return jnp.sum(jnp.where(lane == sub, last, 0.0), axis=1, keepdims=True)


def spread_kernel(x_ref, d_ref, out_ref):
    for j in range(COLS):
        cols = pl.ds(j * CB, CB)
        for c in range(CLASSES):
            out_ref[c * COLS + j, :, :CB] = x_ref[:, cols]
            out_ref[c * COLS + j, :, CB:] = d_ref[:, cols]


def route_kernel(where_ref, ids_ref, slots_ref, probs_ref, hits_ref, weight_ref, pick_ref):
    target = targets(ids_ref[...], slots_ref[...], where_ref[0])
    probs = probs_ref[...].astype(F32)
    row = lax.broadcasted_iota(jnp.int32, (ROWS, TOK), 0)
    hits = jnp.zeros((ROWS, TOK), F32)
    weight = jnp.zeros((ROWS, TOK), F32)
    choice = jnp.zeros((ROWS, TOK), F32)
    for k in range(TOPK):
        hit = row == target[k : k + 1, :]
        hits = jnp.where(hit, 1.0, hits)
        weight = jnp.where(hit, probs[k : k + 1, :], weight)
        choice = jnp.where(hit, float(k), choice)
    lane, sub = row_iotas()
    hits_ref[...] = hits.astype(BF)
    group = spread_column(jnp.sum(weight, axis=1, keepdims=True))
    weight_ref[...] = jnp.where(sub == SLOTS - 1, group, 0.0).astype(BF)
    pick = jnp.sum(choice, axis=1, keepdims=True).astype(jnp.int32)
    pick_ref[...] = jnp.where(lane == pick, 1.0, 0.0).astype(BF)


def dispatch_kernel(hits_ref, weight_ref, tok_ref, out_ref):
    rows = dot(hits_ref[...], tok_ref[...].reshape(TOK, 2 * CB), NN)
    out_ref[:, :LANES] = (rows[:, :LANES] + weight_ref[...].astype(F32)).astype(BF)
    out_ref[:, LANES:] = rows[:, LANES:].astype(BF)


def block_starts(where_ref):
    z, core = where_ref[1], where_ref[2]
    starts = []
    for side in range(CORES):
        c = core if side == 0 else 1 - core
        for step in range(ZL):
            owner = ((z - step + ZL) & (ZL - 1)) * CORES + c
            starts.append(pl.multiple_of(owner * CB, CB))
    return starts


def store_input_grads(out_ref, starts, d_gate, d_up, pair, wg, wu):
    _, sub = row_iotas()
    for i, start in enumerate(starts):
        cols = pl.ds(start, CB)
        out = dot(d_gate, wg[:, cols], NN) + dot(d_up, wu[:, cols], NN)
        head = jnp.where(sub == SLOTS - 1, pair, out[:, :LANES])
        out_ref[i, :, :LANES] = head.astype(out_ref.dtype)
        out_ref[i, :, LANES:] = out[:, LANES:].astype(out_ref.dtype)


def hidden_kernel(where_ref, *refs):
    blocks = refs[: 2 * ZL]
    wg, wu, wd = refs[2 * ZL : 2 * ZL + 3]
    other_ref, gate_ref, up_ref, pair_ref, grads_ref = refs[2 * ZL + 3 :]
    starts = block_starts(where_ref)
    gate = jnp.zeros((ROWS, HID), F32)
    up = jnp.zeros((ROWS, HID), F32)
    back = jnp.zeros((ROWS, HID), F32)
    for block, start in zip(blocks, starts, strict=True):
        cols = pl.ds(start, CB)
        gate += dot(block[:, :CB], wg[:, cols], NT)
        up += dot(block[:, :CB], wu[:, cols], NT)
        back += dot(block[:, CB:], wd[:, cols], NT)
    prob = gather_column(blocks[0][:, :LANES].astype(F32))
    sig = jax.nn.sigmoid(gate)
    act = gate * sig
    hidden = act * up
    pair = spread_column(jnp.sum(hidden * back, axis=1, keepdims=True))
    d_hidden = prob * back
    d_gate = d_hidden * up * sig * (1.0 + gate * (1.0 - sig))
    d_up = d_hidden * act
    scaled = prob * hidden
    grads_ref[0] = d_gate.T.astype(BF)
    grads_ref[1] = d_up.T.astype(BF)
    grads_ref[2] = scaled.T.astype(BF)
    d_gate = d_gate.astype(BF)
    d_up = d_up.astype(BF)
    gate_ref[...] = d_gate
    up_ref[...] = d_up
    pair_ref[...] = pair
    store_input_grads(other_ref, starts[ZL:], d_gate, d_up, pair, wg, wu)


def own_kernel(where_ref, gate_ref, up_ref, pair_ref, wg, wu, out_ref):
    starts = block_starts(where_ref)[:ZL]
    store_input_grads(out_ref, starts, gate_ref[...], up_ref[...], pair_ref[...], wg, wu)


def weight_kernel(where_ref, *refs):
    blocks = refs[: 2 * ZL]
    grads_ref = refs[2 * ZL]
    gate_ref, up_ref, down_ref = refs[2 * ZL + 1 :]
    for block, start in zip(blocks, block_starts(where_ref), strict=True):
        cols = pl.ds(start, CB)
        gate_ref[:, cols] = dot(grads_ref[0], block[:, :CB], NN)
        up_ref[:, cols] = dot(grads_ref[1], block[:, :CB], NN)
        down_ref[:, cols] = dot(grads_ref[2], block[:, CB:], NN)


def combine_kernel(hits_ref, pick_ref, back_ref, out_ref):
    hits = hits_ref[...]
    value = gather_column(back_ref[:, :LANES].astype(F32))
    pairs = (pick_ref[...].astype(F32) * value).astype(BF)
    rows = dot(hits, back_ref[...], TN)
    probs = dot(hits, pairs, TN)
    for i in range(CLASSES * COLS):
        out_ref[i, :, :CB] = rows[2 * i : 2 * i + 2]
        out_ref[i, :, CB:] = probs[2 * i : 2 * i + 2]


def finish_kernel(in_ref, x_ref, p_ref):
    for j in range(COLS):
        total = in_ref[j]
        for c in range(1, CLASSES):
            total += in_ref[c * COLS + j]
        x_ref[:, j * CB : (j + 1) * CB] = total[:, :CB].astype(BF)
        if j == 0:
            p_ref[...] = total[:, CB : CB + TOPK]


VMEM_LIMIT = 16 << 20


def call(kernel, args, outs, scalars=None, near=True, flops=0, moved=0):
    vmem = pl.BlockSpec(memory_space=pltpu.VMEM)
    smem = pl.BlockSpec(memory_space=pltpu.SMEM)
    if near:
        args = [pltpu.with_memory_space_constraint(v, pltpu.VMEM) for v in args]
    in_specs = [vmem] * len(args)
    if scalars is not None:
        args, in_specs = [scalars, *args], [smem, *in_specs]
    return pl.pallas_call(
        kernel,
        out_shape=outs,
        in_specs=in_specs,
        out_specs=jax.tree.map(lambda _: vmem, outs, is_leaf=lambda v: hasattr(v, "dtype")),
        compiler_params=pltpu.CompilerParams(vmem_limit_bytes=VMEM_LIMIT),
        cost_estimate=pl.CostEstimate(flops=flops, bytes_accessed=moved, transcendentals=0),
    )(*args)


def shape(dims, dtype):
    return jax.ShapeDtypeStruct(dims, dtype)


def near(dims, dtype):
    return pltpu.VMEM(dims, dtype)


def exchange(v, axis):
    return lax.all_to_all(v, axis, split_axis=0, concat_axis=0, tiled=True)


def local(tok_x, grad_out, expert_ids, slot_ids, route_probs, gate_weight, up_weight, down_weight):
    place = lax.axis_index("local")
    where = jnp.stack([place // COLS, (place // CORES) % ZL, place % CORES]).astype(jnp.int32)
    wg, wu, wd = gate_weight[0], up_weight[0], down_weight[0]
    own = tok_x.shape[0]
    peers = CLASSES * COLS
    with jax.named_scope("tokens_to_columns"):
        both = call(spread_kernel, [tok_x, grad_out], near((peers, own, 2 * CB), BF))
        tokens = exchange(both, "local")
    with jax.named_scope("routing"):
        hits, weight, pick = call(
            route_kernel,
            [expert_ids.T, slot_ids.T, route_probs.T],
            (near((ROWS, TOK), BF), near((ROWS, LANES), BF), near((ROWS, LANES), BF)),
            scalars=where,
        )
    with jax.named_scope("rows_to_experts"):
        outbox = call(dispatch_kernel, [hits, weight, tokens], near((ROWS, 2 * CB), BF))
        rows = exchange(outbox.reshape(NODES, SLOTS, 2 * CB), "node").reshape(ROWS, 2 * CB)
    with jax.named_scope("gather_columns"):
        mine = [rows] + [
            lax.ppermute(rows, "local", shift_pairs(step)) for step in range(1, ZL)
        ]
        theirs = [lax.ppermute(v, "local", CORE_PAIRS) for v in mine]
    blocks = mine + theirs
    with jax.named_scope("hidden_grads"):
        other, d_gate, d_up, pair, grads = call(
            hidden_kernel,
            [*blocks, wg, wu, wd],
            (
                near((ZL, ROWS, CB), BF),
                near((ROWS, HID), BF),
                near((ROWS, HID), BF),
                near((ROWS, LANES), F32),
                shape((3, HID, ROWS), BF),
            ),
            scalars=where,
            flops=8 * ROWS * HID * D,
            moved=4 << 20,
        )
    with jax.named_scope("scatter_columns"):
        other = lax.ppermute(other, "local", CORE_PAIRS)
        part = call(
            own_kernel,
            [d_gate, d_up, pair, wg, wu],
            near((ZL, ROWS, CB), F32),
            scalars=where,
            flops=2 * ROWS * HID * D,
            moved=2 << 20,
        )
        sums = [part[step] + other[step].astype(F32) for step in range(ZL)]
        moved = [
            lax.ppermute(sums[step].astype(BF), "local", shift_pairs(-step))
            for step in range(1, ZL)
        ]
    with jax.named_scope("weight_grads"):
        weight_grads = call(
            weight_kernel,
            [*blocks, grads],
            (shape((HID, D), F32),) * 3,
            scalars=where,
            near=False,
            flops=6 * ROWS * HID * D,
            moved=5 << 20,
        )
    moved, weight_grads = lax.optimization_barrier((moved, weight_grads))
    with jax.named_scope("rows_to_tokens"):
        total = sums[0]
        for v in moved:
            total += v.astype(F32)
        back = exchange(total.astype(BF).reshape(NODES, SLOTS, CB), "node").reshape(ROWS, CB)
        partial = call(combine_kernel, [hits, pick, back], near((peers, own, CB + LANES), F32))
    with jax.named_scope("columns_to_tokens"):
        pieces = exchange(partial, "local")
        grad_x, grad_p = call(finish_kernel, [pieces], (shape((own, D), BF), shape((own, TOPK), F32)))
    gate_grad, up_grad, down_grad = weight_grads
    return grad_x, grad_p, gate_grad[None], up_grad[None], down_grad[None]


def solution(mesh):
    both = ("node", "local")
    in_specs = (
        P(both, None),
        P(both, None),
        P("node", None),
        P("node", None),
        P("node", None),
        P(both, None, None),
        P(both, None, None),
        P(both, None, None),
    )
    out_specs = (
        P(both, None),
        P(both, None),
        P(both, None, None),
        P(both, None, None),
        P(both, None, None),
    )
    return jax.shard_map(local, mesh=mesh, in_specs=in_specs, out_specs=out_specs, check_vma=False)
```

time: 560 us -> 161 us (0.29); the launches traced: 551 us -> 160 us
  waiting for transfers between devices: 204 us -> 25 us
  blocking collectives: 221 us -> 72.8 us
  starting transfers between devices: 80.6 us -> 51.3 us
  local copies, waits for them, and re-layouts: 23.7 us -> 1.41 us
  matrix products: 14.4 us -> 0 us
  Pallas kernels: 0 us -> 8.49 us
    all_to_all x5 -> x1, waiting for transfers between devices: 204 us -> 6.87 us  [exchange(): return lax.all_to_all(v, axis, split_axis=0, concat_axis=0, tiled=True)]
    unnamed x1 -> x0, blocking collectives: 137 us -> none
    all_gather x2 -> x0, blocking collectives: 84.2 us -> none  [the longest x1 45.1 us: local(): lax.all_gather(tok_x, 'local', axis=0, tiled=True)]
    all_to_all x0 -> x3, blocking collectives: none -> 72.8 us  [exchange(): return lax.all_to_all(v, axis, split_axis=0, concat_axis=0, tiled=True)]
    all_to_all x5 -> x1, starting transfers between devices: 80.6 us -> 17.8 us  [exchange(): return lax.all_to_all(v, axis, split_axis=0, concat_axis=0, tiled=True)]
    ppermute x0 -> x11, starting transfers between devices: none -> 33.5 us  [the longest x4 11.8 us: local(): theirs = [lax.ppermute(v, 'local', CORE_PAIRS) for v in mine]]
    ppermute x0 -> x11, waiting for transfers between devices: none -> 18.1 us  [the longest x3 12.2 us: local(): lax.ppermute(rows, 'local', shift_pairs(step))]
    dot_general x9 -> x0, matrix products: 14.4 us -> none  [the longest x1 2.44 us: owner_grads(): jnp.dot(d_up, w_up_rows, preferred_element_type=jnp.float32)]
  transfers between devices with their start and end apart: 5 -> 12, of which waited for: 4 -> 6; matrix products, arithmetic and copies ran while one was open for 4% -> 0% of each run, Pallas kernels for 0% -> 3%
where the time goes in v1:
time: 161 us; the launch traced here: 160 us
  blocking collectives  72.8 us (45%)
  starting transfers between devices  51.3 us (32%)
  waiting for transfers between devices  25 us (16%)
  Pallas kernels  8.49 us (5%)
    all_to_all x3, blocking collectives, exchange(): return lax.all_to_all(v, axis, split_axis=0, concat_axis=0, tiled=True)  72.8 us
    all_to_all x1, starting transfers between devices, exchange(): return lax.all_to_all(v, axis, split_axis=0, concat_axis=0, tiled=True)  17.8 us
    ppermute x3, waiting for transfers between devices, local(): lax.ppermute(rows, 'local', shift_pairs(step))  12.2 us
    ppermute x4, starting transfers between devices, local(): theirs = [lax.ppermute(v, 'local', CORE_PAIRS) for v in mine]  11.8 us
    ppermute x3, starting transfers between devices, local(): lax.ppermute(rows, 'local', shift_pairs(step))  10.6 us
    ppermute x3, starting transfers between devices, local(): lax.ppermute(sums[step].astype(BF), 'local', shift_pairs(-step))  9 us
    pallas_call x8, Pallas kernels, call(): pl.pallas_call(kernel, out_shape=outs, in_specs=in_specs, out_specs=jax.t...  8.49 us
    all_to_all x1, waiting for transfers between devices, exchange(): return lax.all_to_all(v, axis, split_axis=0, concat_axis=0, tiled=True)  6.87 us
  transfers between devices with their start and end apart: 12, of which 6 were waited for; matrix products, arithmetic and copies ran while one was open for 0% of the time, Pallas kernels for 3%

profile of v1, /device:TPU:1, one launch (start us, length us, event | category | flops | bytes accessed | tf_op | source)
XLA Modules:
  0.0 160.0 jit_solution(10854293501280645626)
XLA Ops:
  2.7 17.8 %all-to-all-start = ((bf16[32,2,512]{2,1,0:T(2,128)(2,1)}), bf16[32,2,512]{2,1,0:T(2,128)(2,1)S(1)}, u32[]{:S(2)}, u32[]{:S(2)}) async-start(bf16[32,2,512]{2,1,0:T(2,128)(2,1)} %tokens_to_columns.1), calls=%async_computation | async-start | bytes 131072 | tf_op jit(solution)/shard_map/tokens_to_columns/all_to_all | solution.py:226
  20.6 0.9 routing.1
  21.5 6.9 %all-to-all-done.tok_ref = bf16[32,2,512]{2,1,0:T(2,128)(2,1)S(1)} async-done(((bf16[32,2,512]{2,1,0:T(2,128)(2,1)}), bf16[32,2,512]{2,1,0:T(2,128)(2,1)S(1)}, u32[]{:S(2)}, u32[]{:S(2)}) %all-to-all-start) | async-done | bytes 65568 | tf_op jit(solution)/shard_map/tokens_to_columns/all_to_all | solution.py:226
  28.6 34.9 %all_to_all.20 = bf16[32,8,512]{2,1,0:T(8,128)(2,1)S(1)} all-to-all(bf16[32,8,512]{2,1,0:T(8,128)(2,1)S(1)} %bitcast.45), channel_id=1, replica_groups=mesh['node'=32,'local'=32] {'node'}, dimensions={0} | all-to-all | bytes 524288 | tf_op jit(solution)/shard_map/rows_to_experts/all_to_all | solution.py:226
  63.5 1.9 %collective-permute-start.2 = (bf16[256,512]{1,0:T(8,128)(2,1)S(1)}, bf16[256,512]{1,0:T(8,128)(2,1)S(1)}, u32[]{:S(2)}, u32[]{:S(2)}) collective-permute-start(bf16[256,512]{1,0:T(8,128)(2,1)S(1)} %bitcast.35), channel_id=1, source_target_pairs={{0,6},{1,7},{2,0},{3,1},{4,2},{5,3},{6,4},{7,5},{8,14},{9,15},{10,... | collective-permute-start | bytes 786440 | tf_op jit(solution)/shard_map/gather_columns/ppermute | solution.py:250
  65.5 6.8 %collective-permute-start.1 = (bf16[256,512]{1,0:T(8,128)(2,1)S(1)}, bf16[256,512]{1,0:T(8,128)(2,1)S(1)}, u32[]{:S(2)}, u32[]{:S(2)}) collective-permute-start(bf16[256,512]{1,0:T(8,128)(2,1)S(1)} %bitcast.36), channel_id=1, source_target_pairs={{0,4},{1,5},{2,6},{3,7},{4,0},{5,1},{6,2},{7,3},{8,12},{9,13},{10,... | collective-permute-start | bytes 786440 | tf_op jit(solution)/shard_map/gather_columns/ppermute | solution.py:250
  72.3 1.9 %collective-permute-start = (bf16[256,512]{1,0:T(8,128)(2,1)S(1)}, bf16[256,512]{1,0:T(8,128)(2,1)S(1)}, u32[]{:S(2)}, u32[]{:S(2)}) collective-permute-start(bf16[256,512]{1,0:T(8,128)(2,1)S(1)} %bitcast.37), channel_id=1, source_target_pairs={{0,2},{1,3},{2,4},{3,5},{4,6},{5,7},{6,0},{7,1},{8,10},{9,11},{10,... | collective-permute-start | bytes 786440 | tf_op jit(solution)/shard_map/gather_columns/ppermute | solution.py:250
  74.2 4.1 %collective-permute-start.3 = (bf16[256,512]{1,0:T(8,128)(2,1)S(1)}, bf16[256,512]{1,0:T(8,128)(2,1)S(1)}, u32[]{:S(2)}, u32[]{:S(2)}) collective-permute-start(bf16[256,512]{1,0:T(8,128)(2,1)S(1)} %bitcast.38), channel_id=1, source_target_pairs={{0,1},{1,0},{2,3},{3,2},{4,5},{5,4},{6,7},{7,6},{8,9},{9,8},{10,11... | collective-permute-start | bytes 786440 | tf_op jit(solution)/shard_map/gather_columns/ppermute | solution.py:252
  78.4 1.9 %collective-permute-start.6 = (bf16[256,512]{1,0:T(8,128)(2,1)S(1)}, bf16[256,512]{1,0:T(8,128)(2,1)S(1)}, u32[]{:S(2)}, u32[]{:S(2)}) collective-permute-start(bf16[256,512]{1,0:T(8,128)(2,1)S(1)} %collective-permute-done.2.refs_3_), channel_id=1, source_target_pairs={{0,1},{1,0},{2,3},{3,2},{4,5},{5,4},{6,7},{7,6},{8,9},{9,8},{10,11... | collective-permute-start | bytes 786440 | tf_op jit(solution)/shard_map/gather_columns/ppermute | solution.py:252
  80.3 12.2 %collective-permute-done.1.refs_2_ = bf16[256,512]{1,0:T(8,128)(2,1)S(1)} collective-permute-done((bf16[256,512]{1,0:T(8,128)(2,1)S(1)}, bf16[256,512]{1,0:T(8,128)(2,1)S(1)}, u32[]{:S(2)}, u32[]{:S(2)}) %collective-permute-start.1) | collective-permute-done | bytes 262176 | tf_op jit(solution)/shard_map/gather_columns/ppermute | solution.py:250
  92.5 3.8 %collective-permute-start.5 = (bf16[256,512]{1,0:T(8,128)(2,1)S(1)}, bf16[256,512]{1,0:T(8,128)(2,1)S(1)}, u32[]{:S(2)}, u32[]{:S(2)}) collective-permute-start(bf16[256,512]{1,0:T(8,128)(2,1)S(1)} %collective-permute-done.1.refs_2_), channel_id=1, source_target_pairs={{0,1},{1,0},{2,3},{3,2},{4,5},{5,4},{6,7},{7,6},{8,9},{9,8},{10,11... | collective-permute-start | bytes 786440 | tf_op jit(solution)/shard_map/gather_columns/ppermute | solution.py:252
  96.4 1.9 %collective-permute-start.4 = (bf16[256,512]{1,0:T(8,128)(2,1)S(1)}, bf16[256,512]{1,0:T(8,128)(2,1)S(1)}, u32[]{:S(2)}, u32[]{:S(2)}) collective-permute-start(bf16[256,512]{1,0:T(8,128)(2,1)S(1)} %collective-permute-done.refs_1_), channel_id=1, source_target_pairs={{0,1},{1,0},{2,3},{3,2},{4,5},{5,4},{6,7},{7,6},{8,9},{9,8},{10,11... | collective-permute-start | bytes 786440 | tf_op jit(solution)/shard_map/gather_columns/ppermute | solution.py:252
  98.3 1.5 collective-permute-done.4.refs_5_
  99.8 2.4 %hidden_grads.1 = (bf16[4,256,256]{2,1,0:T(8,128)(2,1)S(1)}, bf16[256,96]{1,0:T(8,128)(2,1)S(1)}, bf16[256,96]{1,0:T(8,128)(2,1)S(1)}, f32[256,128]{1,0:T(8,128)S(1)}, bf16[3,96,256]{2,1,0:T(8,128)(2,1)S(1)}) custom-call(s32[3]{0:T(128)S(1)} %pad_add_fusion.where_ref, bf16[256,512]{1,0:T(8,128)(2,1)S(1)} %bitcast.39, ...), custom_call_target="tpu_custom_call" | custom-call | flops 402653184 | bytes 4194304 | tf_op jit(solution)/shard_map/hidden_grads/pallas_call | solution.py:207
  102.2 2.0 %collective-permute-start.7 = (bf16[4,256,256]{2,1,0:T(8,128)(2,1)S(1)}, bf16[4,256,256]{2,1,0:T(8,128)(2,1)S(1)}, u32[]{:S(2)}, u32[]{:S(2)}) collective-permute-start(bf16[4,256,256]{2,1,0:T(8,128)(2,1)S(1)} %get-tuple-element.30), channel_id=1, source_target_pairs={{0,1},{1,0},{2,3},{3,2},{4,5},{5,4},{6,7},{7,6},{8,9},{9,8},{10,11... | collective-permute-start | bytes 1572872 | tf_op jit(solution)/shard_map/scatter_columns/ppermute | solution.py:270
  104.2 1.0 scatter_columns.1
  105.2 0.8 collective-permute-done.7
  106.1 1.9 %collective-permute-start.10 = (bf16[256,256]{1,0:T(8,128)(2,1)S(1)}, bf16[256,256]{1,0:T(8,128)(2,1)S(1)}, u32[]{:S(2)}, u32[]{:S(2)}) collective-permute-start(bf16[256,256]{1,0:T(8,128)(2,1)S(1)} %get-tuple-element.43), channel_id=1, source_target_pairs={{0,2},{1,3},{2,4},{3,5},{4,6},{5,7},{6,0},{7,1},{8,10},{9,11},{10,... | collective-permute-start | bytes 393224 | tf_op jit(solution)/shard_map/scatter_columns/ppermute | solution.py:281
  108.0 1.9 %collective-permute-start.9 = (bf16[256,256]{1,0:T(8,128)(2,1)S(1)}, bf16[256,256]{1,0:T(8,128)(2,1)S(1)}, u32[]{:S(2)}, u32[]{:S(2)}) collective-permute-start(bf16[256,256]{1,0:T(8,128)(2,1)S(1)} %get-tuple-element.44), channel_id=1, source_target_pairs={{0,4},{1,5},{2,6},{3,7},{4,0},{5,1},{6,2},{7,3},{8,12},{9,13},{10,... | collective-permute-start | bytes 393224 | tf_op jit(solution)/shard_map/scatter_columns/ppermute | solution.py:281
  110.0 5.2 %collective-permute-start.8 = (bf16[256,256]{1,0:T(8,128)(2,1)S(1)}, bf16[256,256]{1,0:T(8,128)(2,1)S(1)}, u32[]{:S(2)}, u32[]{:S(2)}) collective-permute-start(bf16[256,256]{1,0:T(8,128)(2,1)S(1)} %get-tuple-element.45), channel_id=1, source_target_pairs={{0,6},{1,7},{2,0},{3,1},{4,2},{5,3},{6,4},{7,5},{8,14},{9,15},{10,... | collective-permute-start | bytes 393224 | tf_op jit(solution)/shard_map/scatter_columns/ppermute | solution.py:281
  115.1 2.5 %weight_grads.1 = (f32[96,2048]{1,0:T(8,128)}, f32[96,2048]{1,0:T(8,128)}, f32[96,2048]{1,0:T(8,128)}) custom-call(s32[3]{0:T(128)S(1)} %pad_add_fusion.where_ref, bf16[256,512]{1,0:T(8,128)(2,1)S(1)} %bitcast.40, bf16[256,512]{1,0:T(8,128)(2,1)S(1)} %collective-permute-done.refs_1_, bf16[256,512]{1,0:T(8,128)(2,1)S(1)} %collective-permute-done.1.refs_2_, ...), custom_call_target="tpu_custom_call" | custom-call | flops 301989888 | bytes 5242880 | tf_op jit(solution)/shard_map/weight_grads/pallas_call | solution.py:207
  117.7 3.2 %collective-permute-done.9 = bf16[256,256]{1,0:T(8,128)(2,1)S(1)} collective-permute-done((bf16[256,256]{1,0:T(8,128)(2,1)S(1)}, bf16[256,256]{1,0:T(8,128)(2,1)S(1)}, u32[]{:S(2)}, u32[]{:S(2)}) %collective-permute-start.9) | collective-permute-done | bytes 131104 | tf_op jit(solution)/shard_map/scatter_columns/ppermute | solution.py:281
  121.4 21.5 %all_to_all.21 = bf16[32,8,256]{2,1,0:T(8,128)(2,1)S(1)} all-to-all(bf16[32,8,256]{2,1,0:T(8,128)(2,1)S(1)} %fusion.8), channel_id=1, replica_groups=mesh['node'=32,'local'=32] {'node'}, dimensions={0} | all-to-all | bytes 262144 | tf_op jit(solution)/shard_map/rows_to_tokens/all_to_all | solution.py:226
  143.2 16.3 %all_to_all.22.in_ref = f32[32,2,384]{2,1,0:T(2,128)S(1)} all-to-all(f32[32,2,384]{2,1,0:T(2,128)S(1)} %rows_to_tokens.1), channel_id=1, replica_groups=mesh['node'=32,'local'=32] {'local'}, dimensions={0} | all-to-all | bytes 196608 | tf_op jit(solution)/shard_map/columns_to_tokens/all_to_all | solution.py:226
  (30 shorter events, 3.7 us)
Async XLA Ops:
  0.6 0.7 copy-start.3
  1.3 0.7 copy-start.4
  2.0 18.6 %copy-start.5 = (s32[64,8]{0,1:T(8,128)S(1)}, s32[64,8]{0,1:T(8,128)}, u32[]{:S(2)}) copy-start(s32[64,8]{0,1:T(8,128)} %param.10) | copy-start | bytes 6148
  2.0 18.6 %copy-start.6 = (s32[64,8]{0,1:T(8,128)S(1)}, s32[64,8]{0,1:T(8,128)}, u32[]{:S(2)}) copy-start(s32[64,8]{0,1:T(8,128)} %param.11) | copy-start | bytes 6148
  2.0 18.6 %copy-start.7 = (bf16[64,8]{0,1:T(8,128)(2,1)S(1)}, bf16[64,8]{0,1:T(8,128)(2,1)}, u32[]{:S(2)}) copy-start(bf16[64,8]{0,1:T(8,128)(2,1)} %param.12) | copy-start | bytes 3076
  2.7 97.1 %copy-start.2 = (bf16[1,96,2048]{2,1,0:T(8,128)(2,1)S(1)}, bf16[1,96,2048]{2,1,0:T(8,128)(2,1)}, u32[]{:S(2)}) copy-start(bf16[1,96,2048]{2,1,0:T(8,128)(2,1)} %param.15) | copy-start | bytes 1179652
  2.7 25.7 %all-to-all-start = ((bf16[32,2,512]{2,1,0:T(2,128)(2,1)}), bf16[32,2,512]{2,1,0:T(2,128)(2,1)S(1)}, u32[]{:S(2)}, u32[]{:S(2)}) async-start(bf16[32,2,512]{2,1,0:T(2,128)(2,1)} %tokens_to_columns.1), calls=%async_computation | async-start | bytes 131072 | tf_op jit(solution)/shard_map/tokens_to_columns/all_to_all | solution.py:226
  28.4 71.4 %copy-start = (bf16[1,96,2048]{2,1,0:T(8,128)(2,1)S(1)}, bf16[1,96,2048]{2,1,0:T(8,128)(2,1)}, u32[]{:S(2)}) copy-start(bf16[1,96,2048]{2,1,0:T(8,128)(2,1)} %param.13) | copy-start | bytes 1179652
  28.4 71.4 %copy-start.1 = (bf16[1,96,2048]{2,1,0:T(8,128)(2,1)S(1)}, bf16[1,96,2048]{2,1,0:T(8,128)(2,1)}, u32[]{:S(2)}) copy-start(bf16[1,96,2048]{2,1,0:T(8,128)(2,1)} %param.14) | copy-start | bytes 1179652
  63.5 14.8 %collective-permute-start.2 = (bf16[256,512]{1,0:T(8,128)(2,1)S(1)}, bf16[256,512]{1,0:T(8,128)(2,1)S(1)}, u32[]{:S(2)}, u32[]{:S(2)}) collective-permute-start(bf16[256,512]{1,0:T(8,128)(2,1)S(1)} %bitcast.35), channel_id=1, source_target_pairs={{0,6},{1,7},{2,0},{3,1},{4,2},{5,3},{6,4},{7,5},{8,14},{9,15},{10,... | collective-permute-start | bytes 786440 | tf_op jit(solution)/shard_map/gather_columns/ppermute | solution.py:250
  65.5 27.1 %collective-permute-start.1 = (bf16[256,512]{1,0:T(8,128)(2,1)S(1)}, bf16[256,512]{1,0:T(8,128)(2,1)S(1)}, u32[]{:S(2)}, u32[]{:S(2)}) collective-permute-start(bf16[256,512]{1,0:T(8,128)(2,1)S(1)} %bitcast.36), channel_id=1, source_target_pairs={{0,4},{1,5},{2,6},{3,7},{4,0},{5,1},{6,2},{7,3},{8,12},{9,13},{10,... | collective-permute-start | bytes 786440 | tf_op jit(solution)/shard_map/gather_columns/ppermute | solution.py:250
  72.3 24.1 %collective-permute-start = (bf16[256,512]{1,0:T(8,128)(2,1)S(1)}, bf16[256,512]{1,0:T(8,128)(2,1)S(1)}, u32[]{:S(2)}, u32[]{:S(2)}) collective-permute-start(bf16[256,512]{1,0:T(8,128)(2,1)S(1)} %bitcast.37), channel_id=1, source_target_pairs={{0,2},{1,3},{2,4},{3,5},{4,6},{5,7},{6,0},{7,1},{8,10},{9,11},{10,... | collective-permute-start | bytes 786440 | tf_op jit(solution)/shard_map/gather_columns/ppermute | solution.py:250
  74.2 24.1 %collective-permute-start.3 = (bf16[256,512]{1,0:T(8,128)(2,1)S(1)}, bf16[256,512]{1,0:T(8,128)(2,1)S(1)}, u32[]{:S(2)}, u32[]{:S(2)}) collective-permute-start(bf16[256,512]{1,0:T(8,128)(2,1)S(1)} %bitcast.38), channel_id=1, source_target_pairs={{0,1},{1,0},{2,3},{3,2},{4,5},{5,4},{6,7},{7,6},{8,9},{9,8},{10,11... | collective-permute-start | bytes 786440 | tf_op jit(solution)/shard_map/gather_columns/ppermute | solution.py:252
  78.4 19.9 %collective-permute-start.6 = (bf16[256,512]{1,0:T(8,128)(2,1)S(1)}, bf16[256,512]{1,0:T(8,128)(2,1)S(1)}, u32[]{:S(2)}, u32[]{:S(2)}) collective-permute-start(bf16[256,512]{1,0:T(8,128)(2,1)S(1)} %collective-permute-done.2.refs_3_), channel_id=1, source_target_pairs={{0,1},{1,0},{2,3},{3,2},{4,5},{5,4},{6,7},{7,6},{8,9},{9,8},{10,11... | collective-permute-start | bytes 786440 | tf_op jit(solution)/shard_map/gather_columns/ppermute | solution.py:252
  92.5 5.8 %collective-permute-start.5 = (bf16[256,512]{1,0:T(8,128)(2,1)S(1)}, bf16[256,512]{1,0:T(8,128)(2,1)S(1)}, u32[]{:S(2)}, u32[]{:S(2)}) collective-permute-start(bf16[256,512]{1,0:T(8,128)(2,1)S(1)} %collective-permute-done.1.refs_2_), channel_id=1, source_target_pairs={{0,1},{1,0},{2,3},{3,2},{4,5},{5,4},{6,7},{7,6},{8,9},{9,8},{10,11... | collective-permute-start | bytes 786440 | tf_op jit(solution)/shard_map/gather_columns/ppermute | solution.py:252
  96.4 3.4 %collective-permute-start.4 = (bf16[256,512]{1,0:T(8,128)(2,1)S(1)}, bf16[256,512]{1,0:T(8,128)(2,1)S(1)}, u32[]{:S(2)}, u32[]{:S(2)}) collective-permute-start(bf16[256,512]{1,0:T(8,128)(2,1)S(1)} %collective-permute-done.refs_1_), channel_id=1, source_target_pairs={{0,1},{1,0},{2,3},{3,2},{4,5},{5,4},{6,7},{7,6},{8,9},{9,8},{10,11... | collective-permute-start | bytes 786440 | tf_op jit(solution)/shard_map/gather_columns/ppermute | solution.py:252
  102.2 3.8 %collective-permute-start.7 = (bf16[4,256,256]{2,1,0:T(8,128)(2,1)S(1)}, bf16[4,256,256]{2,1,0:T(8,128)(2,1)S(1)}, u32[]{:S(2)}, u32[]{:S(2)}) collective-permute-start(bf16[4,256,256]{2,1,0:T(8,128)(2,1)S(1)} %get-tuple-element.30), channel_id=1, source_target_pairs={{0,1},{1,0},{2,3},{3,2},{4,5},{5,4},{6,7},{7,6},{8,9},{9,8},{10,11... | collective-permute-start | bytes 1572872 | tf_op jit(solution)/shard_map/scatter_columns/ppermute | solution.py:270
  106.1 11.6 %collective-permute-start.10 = (bf16[256,256]{1,0:T(8,128)(2,1)S(1)}, bf16[256,256]{1,0:T(8,128)(2,1)S(1)}, u32[]{:S(2)}, u32[]{:S(2)}) collective-permute-start(bf16[256,256]{1,0:T(8,128)(2,1)S(1)} %get-tuple-element.43), channel_id=1, source_target_pairs={{0,2},{1,3},{2,4},{3,5},{4,6},{5,7},{6,0},{7,1},{8,10},{9,11},{10,... | collective-permute-start | bytes 393224 | tf_op jit(solution)/shard_map/scatter_columns/ppermute | solution.py:281
  108.0 12.9 %collective-permute-start.9 = (bf16[256,256]{1,0:T(8,128)(2,1)S(1)}, bf16[256,256]{1,0:T(8,128)(2,1)S(1)}, u32[]{:S(2)}, u32[]{:S(2)}) collective-permute-start(bf16[256,256]{1,0:T(8,128)(2,1)S(1)} %get-tuple-element.44), channel_id=1, source_target_pairs={{0,4},{1,5},{2,6},{3,7},{4,0},{5,1},{6,2},{7,3},{8,12},{9,13},{10,... | collective-permute-start | bytes 393224 | tf_op jit(solution)/shard_map/scatter_columns/ppermute | solution.py:281
  110.0 11.3 %collective-permute-start.8 = (bf16[256,256]{1,0:T(8,128)(2,1)S(1)}, bf16[256,256]{1,0:T(8,128)(2,1)S(1)}, u32[]{:S(2)}, u32[]{:S(2)}) collective-permute-start(bf16[256,256]{1,0:T(8,128)(2,1)S(1)} %get-tuple-element.45), channel_id=1, source_target_pairs={{0,6},{1,7},{2,0},{3,1},{4,2},{5,3},{6,4},{7,5},{8,14},{9,15},{10,... | collective-permute-start | bytes 393224 | tf_op jit(solution)/shard_map/scatter_columns/ppermute | solution.py:281

commit v2 on v1

--- a/solution.py
+++ b/solution.py
@@ -18,6 +18,8 @@
 D = 2048
 CB = D // COLS
 HID = 96
+PAIR = CORES * HID
+PRE = 640
 LANES = 128
 BF = jnp.bfloat16
 F32 = jnp.float32
@@ -113,30 +115,55 @@
     return starts
 
 
-def store_input_grads(out_ref, starts, d_gate, d_up, pair, wg, wu):
-    _, sub = row_iotas()
-    for i, start in enumerate(starts):
+def core_starts(where_ref):
+    z = where_ref[1]
+    return [
+        pl.multiple_of(((z - step + ZL) & (ZL - 1)) * CB, CB) for step in range(ZL)
+    ]
+
+
+def lend_kernel(where_ref, wg, wu, wd, out_ref):
+    other = 1 - where_ref[2]
+    for i, w in enumerate((wg, wu, wd)):
+        for z in range(ZL):
+            cols = pl.ds(pl.multiple_of((z * CORES + other) * CB, CB), CB)
+            out_ref[i * HID : (i + 1) * HID, z * CB : (z + 1) * CB] = w[:, cols]
+
+
+def stack_kernel(where_ref, wg, wu, wd, lent, into_ref, down_ref):
+    core = where_ref[2]
+    for i, (w, ref, base) in enumerate(
+        ((wg, into_ref, 0), (wu, into_ref, PAIR), (wd, down_ref, 0))
+    ):
+        mine = pl.ds(pl.multiple_of(base + core * HID, HID // 3), HID)
+        theirs = pl.ds(pl.multiple_of(base + (1 - core) * HID, HID // 3), HID)
+        ref[theirs, :] = lent[i * HID : (i + 1) * HID, :]
+        for z in range(ZL):
+            cols = pl.ds(pl.multiple_of((z * CORES + core) * CB, CB), CB)
+            ref[mine, z * CB : (z + 1) * CB] = w[:, cols]
+
+
+def partial_kernel(where_ref, *refs):
+    blocks = refs[:ZL]
+    into, down, out_ref, stacked_ref = refs[ZL:]
+    first = jnp.zeros((ROWS, 2 * PAIR), F32)
+    last = jnp.zeros((ROWS, PAIR), F32)
+    for block, start in zip(blocks, core_starts(where_ref), strict=True):
         cols = pl.ds(start, CB)
-        out = dot(d_gate, wg[:, cols], NN) + dot(d_up, wu[:, cols], NN)
-        head = jnp.where(sub == SLOTS - 1, pair, out[:, :LANES])
-        out_ref[i, :, :LANES] = head.astype(out_ref.dtype)
-        out_ref[i, :, LANES:] = out[:, LANES:].astype(out_ref.dtype)
-
-
-def hidden_kernel(where_ref, *refs):
-    blocks = refs[: 2 * ZL]
-    wg, wu, wd = refs[2 * ZL : 2 * ZL + 3]
-    other_ref, gate_ref, up_ref, pair_ref, grads_ref = refs[2 * ZL + 3 :]
-    starts = block_starts(where_ref)
-    gate = jnp.zeros((ROWS, HID), F32)
-    up = jnp.zeros((ROWS, HID), F32)
-    back = jnp.zeros((ROWS, HID), F32)
-    for block, start in zip(blocks, starts, strict=True):
-        cols = pl.ds(start, CB)
-        gate += dot(block[:, :CB], wg[:, cols], NT)
-        up += dot(block[:, :CB], wu[:, cols], NT)
-        back += dot(block[:, CB:], wd[:, cols], NT)
-    prob = gather_column(blocks[0][:, :LANES].astype(F32))
+        first += dot(block[:, :CB], into[:, cols], NT)
+        last += dot(block[:, CB:], down[:, cols], NT)
+    out_ref[:, : 2 * PAIR] = first
+    out_ref[:, 2 * PAIR : 3 * PAIR] = last
+    out_ref[:, 3 * PAIR :] = jnp.zeros((ROWS, PRE - 3 * PAIR), F32)
+    for step, block in enumerate(blocks):
+        stacked_ref[step] = block[...]
+
+
+def hidden_kernel(where_ref, half_ref, other_ref, rows_ref, into, *outs):
+    grads_ref, own_ref = outs[:2]
+    pre = half_ref[...] + other_ref[...]
+    gate, up, back = pre[:, :PAIR], pre[:, PAIR : 2 * PAIR], pre[:, 2 * PAIR : 3 * PAIR]
+    prob = gather_column(rows_ref[:, :LANES].astype(F32))
     sig = jax.nn.sigmoid(gate)
     act = gate * sig
     hidden = act * up
@@ -145,31 +172,29 @@
     d_gate = d_hidden * up * sig * (1.0 + gate * (1.0 - sig))
     d_up = d_hidden * act
     scaled = prob * hidden
+    _, sub = row_iotas()
+    gate_bf, up_bf = d_gate.astype(BF), d_up.astype(BF)
+    for ref, start in zip((own_ref, *outs[2:]), core_starts(where_ref), strict=True):
+        cols = pl.ds(start, CB)
+        out = dot(gate_bf, into[:PAIR, cols], NN) + dot(up_bf, into[PAIR:, cols], NN)
+        head = jnp.where(sub == SLOTS - 1, pair, out[:, :LANES])
+        ref[:, :LANES] = head.astype(ref.dtype)
+        ref[:, LANES:] = out[:, LANES:].astype(ref.dtype)
     grads_ref[0] = d_gate.T.astype(BF)
     grads_ref[1] = d_up.T.astype(BF)
     grads_ref[2] = scaled.T.astype(BF)
-    d_gate = d_gate.astype(BF)
-    d_up = d_up.astype(BF)
-    gate_ref[...] = d_gate
-    up_ref[...] = d_up
-    pair_ref[...] = pair
-    store_input_grads(other_ref, starts[ZL:], d_gate, d_up, pair, wg, wu)
-
-
-def own_kernel(where_ref, gate_ref, up_ref, pair_ref, wg, wu, out_ref):
-    starts = block_starts(where_ref)[:ZL]
-    store_input_grads(out_ref, starts, gate_ref[...], up_ref[...], pair_ref[...], wg, wu)
 
 
 def weight_kernel(where_ref, *refs):
-    blocks = refs[: 2 * ZL]
-    grads_ref = refs[2 * ZL]
-    gate_ref, up_ref, down_ref = refs[2 * ZL + 1 :]
+    blocks = [*refs[:ZL], *(refs[ZL].at[step] for step in range(ZL))]
+    grads_ref, gate_ref, up_ref, down_ref = refs[ZL + 1 :]
+    mine = pl.ds(pl.multiple_of(where_ref[2] * HID, HID // 3), HID)
+    d_gate, d_up, scaled = (grads_ref[i, mine, :] for i in range(3))
     for block, start in zip(blocks, block_starts(where_ref), strict=True):
         cols = pl.ds(start, CB)
-        gate_ref[:, cols] = dot(grads_ref[0], block[:, :CB], NN)
-        up_ref[:, cols] = dot(grads_ref[1], block[:, :CB], NN)
-        down_ref[:, cols] = dot(grads_ref[2], block[:, CB:], NN)
+        gate_ref[:, cols] = dot(d_gate, block[:, :CB], NN)
+        up_ref[:, cols] = dot(d_up, block[:, :CB], NN)
+        down_ref[:, cols] = dot(scaled, block[:, CB:], NN)
 
 
 def combine_kernel(hits_ref, pick_ref, back_ref, out_ref):
@@ -196,11 +221,12 @@
 VMEM_LIMIT = 16 << 20
 
 
-def call(kernel, args, outs, scalars=None, near=True, flops=0, moved=0):
+def call(kernel, args, outs, scalars=None, inside=True, flops=0, moved=0):
     vmem = pl.BlockSpec(memory_space=pltpu.VMEM)
     smem = pl.BlockSpec(memory_space=pltpu.SMEM)
-    if near:
-        args = [pltpu.with_memory_space_constraint(v, pltpu.VMEM) for v in args]
+    if inside is not None:
+        space = pltpu.VMEM if inside else pltpu.HBM
+        args = [pltpu.with_memory_space_constraint(v, space) for v in args]
     in_specs = [vmem] * len(args)
     if scalars is not None:
         args, in_specs = [scalars, *args], [smem, *in_specs]
@@ -233,13 +259,22 @@
     own = tok_x.shape[0]
     peers = CLASSES * COLS
     with jax.named_scope("tokens_to_columns"):
-        both = call(spread_kernel, [tok_x, grad_out], near((peers, own, 2 * CB), BF))
+        both = call(spread_kernel, [tok_x, grad_out], near((peers, own, 2 * CB), BF), inside=False)
         tokens = exchange(both, "local")
     with jax.named_scope("routing"):
         hits, weight, pick = call(
             route_kernel,
             [expert_ids.T, slot_ids.T, route_probs.T],
             (near((ROWS, TOK), BF), near((ROWS, LANES), BF), near((ROWS, LANES), BF)),
+            scalars=where,
+        )
+    with jax.named_scope("core_weights"):
+        lent = call(lend_kernel, [wg, wu, wd], near((3 * HID, ZL * CB), BF), scalars=where)
+        lent = lax.ppermute(lent, "local", CORE_PAIRS)
+        into, down = call(
+            stack_kernel,
+            [wg, wu, wd, lent],
+            (near((2 * PAIR, ZL * CB), BF), near((PAIR, ZL * CB), BF)),
             scalars=where,
         )
     with jax.named_scope("rows_to_experts"):
@@ -249,51 +284,42 @@
         mine = [rows] + [
             lax.ppermute(rows, "local", shift_pairs(step)) for step in range(1, ZL)
         ]
-        theirs = [lax.ppermute(v, "local", CORE_PAIRS) for v in mine]
-    blocks = mine + theirs
     with jax.named_scope("hidden_grads"):
-        other, d_gate, d_up, pair, grads = call(
+        half, stacked = call(
+            partial_kernel,
+            [*mine, into, down],
+            (near((ROWS, PRE), F32), near((ZL, ROWS, 2 * CB), BF)),
+            scalars=where,
+            flops=6 * ROWS * HID * D,
+            moved=3 << 20,
+        )
+        other = lax.ppermute(half, "local", CORE_PAIRS)
+        grads, total, *sums = call(
             hidden_kernel,
-            [*blocks, wg, wu, wd],
-            (
-                near((ZL, ROWS, CB), BF),
-                near((ROWS, HID), BF),
-                near((ROWS, HID), BF),
-                near((ROWS, LANES), F32),
-                shape((3, HID, ROWS), BF),
-            ),
-            scalars=where,
-            flops=8 * ROWS * HID * D,
-            moved=4 << 20,
+            [half, other, rows, into],
+            (shape((3, PAIR, ROWS), BF), near((ROWS, CB), F32)) + (near((ROWS, CB), BF),) * (ZL - 1),
+            scalars=where,
+            flops=4 * ROWS * HID * D,
+            moved=2 << 20,
         )
     with jax.named_scope("scatter_columns"):
-        other = lax.ppermute(other, "local", CORE_PAIRS)
-        part = call(
-            own_kernel,
-            [d_gate, d_up, pair, wg, wu],
-            near((ZL, ROWS, CB), F32),
-            scalars=where,
-            flops=2 * ROWS * HID * D,
-            moved=2 << 20,
-        )
-        sums = [part[step] + other[step].astype(F32) for step in range(ZL)]
         moved = [
-            lax.ppermute(sums[step].astype(BF), "local", shift_pairs(-step))
-            for step in range(1, ZL)
+            lax.ppermute(v, "local", shift_pairs(-step)) for step, v in enumerate(sums, start=1)
         ]
+        stacked, sums = lax.optimization_barrier((stacked, sums))
+        theirs = lax.ppermute(stacked, "local", CORE_PAIRS)
     with jax.named_scope("weight_grads"):
         weight_grads = call(
             weight_kernel,
-            [*blocks, grads],
+            [*mine, theirs, grads],
             (shape((HID, D), F32),) * 3,
             scalars=where,
-            near=False,
+            inside=None,
             flops=6 * ROWS * HID * D,
             moved=5 << 20,
         )
     moved, weight_grads = lax.optimization_barrier((moved, weight_grads))
     with jax.named_scope("rows_to_tokens"):
-        total = sums[0]
         for v in moved:
             total += v.astype(F32)
         back = exchange(total.astype(BF).reshape(NODES, SLOTS, CB), "node").reshape(ROWS, CB)

time: 161 us -> 157 us (0.975)
  blocking collectives: 72.8 us -> 37 us
  waiting for transfers between devices: 25 us -> 48.4 us
  starting transfers between devices: 51.3 us -> 59.4 us
  Pallas kernels: 8.49 us -> 10.2 us
    all_to_all x3 -> x2, blocking collectives: 72.8 us -> 37 us  [exchange(): return lax.all_to_all(v, axis, split_axis=0, concat_axis=0, tiled=True)]
    all_to_all x1 -> x2, waiting for transfers between devices: 6.87 us -> 23.5 us  [exchange(): return lax.all_to_all(v, axis, split_axis=0, concat_axis=0, tiled=True)]
    all_to_all x1 -> x2, starting transfers between devices: 17.8 us -> 32.8 us  [exchange(): return lax.all_to_all(v, axis, split_axis=0, concat_axis=0, tiled=True)]
    ppermute x8 -> x6, starting transfers between devices: 22.8 us -> 16 us  [the longest x3 7.2 us: local(): lax.ppermute(v, 'local', shift_pairs(-step))]
    ppermute x3, waiting for transfers between devices: 12.2 us -> 17.6 us  [local(): lax.ppermute(rows, 'local', shift_pairs(step))]
    pallas_call x8 -> x10, Pallas kernels: 8.49 us -> 10.2 us  [call(): pl.pallas_call(kernel, out_shape=outs, in_specs=in_specs, out_specs=jax.t...]
    ppermute x8 -> x6, waiting for transfers between devices: 5.88 us -> 7.23 us  [the longest x3 5.52 us: local(): lax.ppermute(v, 'local', shift_pairs(-step))]
  transfers between devices with their start and end apart: 12 -> 11, of which waited for: 6 -> 5; matrix products, arithmetic and copies ran while one was open for 0% -> 0% of each run, Pallas kernels for 3% -> 3%
where the time goes in v2:
time: 157 us; the launch traced here: 156 us
  starting transfers between devices  59.4 us (38%)
  waiting for transfers between devices  48.4 us (31%)
  blocking collectives  37 us (24%)
  Pallas kernels  10.2 us (6%)
    all_to_all x2, blocking collectives, exchange(): return lax.all_to_all(v, axis, split_axis=0, concat_axis=0, tiled=True)  37 us
    all_to_all x2, starting transfers between devices, exchange(): return lax.all_to_all(v, axis, split_axis=0, concat_axis=0, tiled=True)  32.8 us
    all_to_all x2, waiting for transfers between devices, exchange(): return lax.all_to_all(v, axis, split_axis=0, concat_axis=0, tiled=True)  23.5 us
    ppermute x3, waiting for transfers between devices, local(): lax.ppermute(rows, 'local', shift_pairs(step))  17.6 us
    ppermute x3, starting transfers between devices, local(): lax.ppermute(rows, 'local', shift_pairs(step))  10.6 us
    pallas_call x10, Pallas kernels, call(): pl.pallas_call(kernel, out_shape=outs, in_specs=in_specs, out_specs=jax.t...  10.2 us
    ppermute x3, starting transfers between devices, local(): lax.ppermute(v, 'local', shift_pairs(-step))  7.2 us
    ppermute x3, waiting for transfers between devices, local(): lax.ppermute(v, 'local', shift_pairs(-step))  5.52 us
  transfers between devices with their start and end apart: 11, of which 5 were waited for; matrix products, arithmetic and copies ran while one was open for 0% of the time, Pallas kernels for 3%

profile of v2, /device:TPU:1, one launch (start us, length us, event | category | flops | bytes accessed | tf_op | source)
XLA Modules:
  0.0 156.1 jit_solution(7381621972070079764)
XLA Ops:
  0.7 1.4 tokens_to_columns.1
  2.0 17.8 %all-to-all-start = ((bf16[32,2,512]{2,1,0:T(2,128)(2,1)}), bf16[32,2,512]{2,1,0:T(2,128)(2,1)S(1)}, u32[]{:S(2)}, u32[]{:S(2)}) async-start(bf16[32,2,512]{2,1,0:T(2,128)(2,1)} %tokens_to_columns.1), calls=%async_computation | async-start | bytes 131072 | tf_op jit(solution)/shard_map/tokens_to_columns/all_to_all | solution.py:252
  20.0 0.9 routing.1
  20.9 6.9 %all-to-all-done.tok_ref = bf16[32,2,512]{2,1,0:T(2,128)(2,1)S(1)} async-done(((bf16[32,2,512]{2,1,0:T(2,128)(2,1)}), bf16[32,2,512]{2,1,0:T(2,128)(2,1)S(1)}, u32[]{:S(2)}, u32[]{:S(2)}) %all-to-all-start) | async-done | bytes 65568 | tf_op jit(solution)/shard_map/tokens_to_columns/all_to_all | solution.py:252
  27.7 0.9 rows_to_experts.1
  28.7 15.0 %all-to-all-start.1 = ((bf16[32,8,512]{2,1,0:T(8,128)(2,1)}), bf16[32,8,512]{2,1,0:T(8,128)(2,1)S(1)}, u32[]{:S(2)}, u32[]{:S(2)}) async-start(bf16[32,8,512]{2,1,0:T(8,128)(2,1)} %bitcast.6), calls=%async_computation.1 | async-start | bytes 524288 | tf_op jit(solution)/shard_map/rows_to_experts/all_to_all | solution.py:252
  44.3 2.7 %collective-permute-start.3 = (bf16[288,1024]{1,0:T(8,128)(2,1)S(1)}, bf16[288,1024]{1,0:T(8,128)(2,1)S(1)}, u32[]{:S(2)}, u32[]{:S(2)}) collective-permute-start(bf16[288,1024]{1,0:T(8,128)(2,1)S(1)} %core_weights.2), channel_id=1, source_target_pairs={{0,1},{1,0},{2,3},{3,2},{4,5},{5,4},{6,7},{7,6},{8,9},{9,8},{10,11... | collective-permute-start | bytes 1769480 | tf_op jit(solution)/shard_map/core_weights/ppermute | solution.py:273
  47.0 16.7 %all-to-all-done.1 = bf16[32,8,512]{2,1,0:T(8,128)(2,1)S(1)} async-done(((bf16[32,8,512]{2,1,0:T(8,128)(2,1)}), bf16[32,8,512]{2,1,0:T(8,128)(2,1)S(1)}, u32[]{:S(2)}, u32[]{:S(2)}) %all-to-all-start.1) | async-done | bytes 262176 | tf_op jit(solution)/shard_map/rows_to_experts/all_to_all | solution.py:252
  63.7 1.9 %collective-permute-start.2 = (bf16[256,512]{1,0:T(8,128)(2,1)S(1)}, bf16[256,512]{1,0:T(8,128)(2,1)S(1)}, u32[]{:S(2)}, u32[]{:S(2)}) collective-permute-start(bf16[256,512]{1,0:T(8,128)(2,1)S(1)} %bitcast.17), channel_id=1, source_target_pairs={{0,6},{1,7},{2,0},{3,1},{4,2},{5,3},{6,4},{7,5},{8,14},{9,15},{10,... | collective-permute-start | bytes 786440 | tf_op jit(solution)/shard_map/gather_columns/ppermute | solution.py:285
  65.6 6.8 %collective-permute-start.1 = (bf16[256,512]{1,0:T(8,128)(2,1)S(1)}, bf16[256,512]{1,0:T(8,128)(2,1)S(1)}, u32[]{:S(2)}, u32[]{:S(2)}) collective-permute-start(bf16[256,512]{1,0:T(8,128)(2,1)S(1)} %bitcast.18), channel_id=1, source_target_pairs={{0,4},{1,5},{2,6},{3,7},{4,0},{5,1},{6,2},{7,3},{8,12},{9,13},{10,... | collective-permute-start | bytes 786440 | tf_op jit(solution)/shard_map/gather_columns/ppermute | solution.py:285
  72.4 1.9 %collective-permute-start = (bf16[256,512]{1,0:T(8,128)(2,1)S(1)}, bf16[256,512]{1,0:T(8,128)(2,1)S(1)}, u32[]{:S(2)}, u32[]{:S(2)}) collective-permute-start(bf16[256,512]{1,0:T(8,128)(2,1)S(1)} %bitcast.19), channel_id=1, source_target_pairs={{0,2},{1,3},{2,4},{3,5},{4,6},{5,7},{6,0},{7,1},{8,10},{9,11},{10,... | collective-permute-start | bytes 786440 | tf_op jit(solution)/shard_map/gather_columns/ppermute | solution.py:285
  75.0 17.6 %collective-permute-done.1.refs_2_ = bf16[256,512]{1,0:T(8,128)(2,1)S(1)} collective-permute-done((bf16[256,512]{1,0:T(8,128)(2,1)S(1)}, bf16[256,512]{1,0:T(8,128)(2,1)S(1)}, u32[]{:S(2)}, u32[]{:S(2)}) %collective-permute-start.1) | collective-permute-done | bytes 262176 | tf_op jit(solution)/shard_map/gather_columns/ppermute | solution.py:285
  92.7 1.2 hidden_grads.2
  93.8 3.8 %collective-permute-start.4 = (f32[256,640]{1,0:T(8,128)S(1)}, f32[256,640]{1,0:T(8,128)S(1)}, u32[]{:S(2)}, u32[]{:S(2)}) collective-permute-start(f32[256,640]{1,0:T(8,128)S(1)} %get-tuple-element.34.half_ref), channel_id=1, source_target_pairs={{0,1},{1,0},{2,3},{3,2},{4,5},{5,4},{6,7},{7,6},{8,9},{9,8},{10,11... | collective-permute-start | bytes 1966088 | tf_op jit(solution)/shard_map/hidden_grads/ppermute | solution.py:296
  97.7 1.7 %collective-permute-done.4.other_ref = f32[256,640]{1,0:T(8,128)S(1)} collective-permute-done((f32[256,640]{1,0:T(8,128)S(1)}, f32[256,640]{1,0:T(8,128)S(1)}, u32[]{:S(2)}, u32[]{:S(2)}) %collective-permute-start.4) | collective-permute-done | bytes 655392 | tf_op jit(solution)/shard_map/hidden_grads/ppermute | solution.py:296
  99.4 1.2 hidden_grads.3
  100.6 2.3 %collective-permute-start.8 = (bf16[4,256,512]{2,1,0:T(8,128)(2,1)S(1)}, bf16[4,256,512]{2,1,0:T(8,128)(2,1)S(1)}, u32[]{:S(2)}, u32[]{:S(2)}) collective-permute-start(bf16[4,256,512]{2,1,0:T(8,128)(2,1)S(1)} %get-tuple-element.40), channel_id=1, source_target_pairs={{0,1},{1,0},{2,3},{3,2},{4,5},{5,4},{6,7},{7,6},{8,9},{9,8},{10,11... | collective-permute-start | bytes 3145736 | tf_op jit(solution)/shard_map/scatter_columns/ppermute | solution.py:310
  102.8 1.9 %collective-permute-start.5 = (bf16[256,256]{1,0:T(8,128)(2,1)S(1)}, bf16[256,256]{1,0:T(8,128)(2,1)S(1)}, u32[]{:S(2)}, u32[]{:S(2)}) collective-permute-start(bf16[256,256]{1,0:T(8,128)(2,1)S(1)} %get-tuple-element.36), channel_id=1, source_target_pairs={{0,6},{1,7},{2,0},{3,1},{4,2},{5,3},{6,4},{7,5},{8,14},{9,15},{10,... | collective-permute-start | bytes 393224 | tf_op jit(solution)/shard_map/scatter_columns/ppermute | solution.py:307
  104.8 1.9 %collective-permute-start.6 = (bf16[256,256]{1,0:T(8,128)(2,1)S(1)}, bf16[256,256]{1,0:T(8,128)(2,1)S(1)}, u32[]{:S(2)}, u32[]{:S(2)}) collective-permute-start(bf16[256,256]{1,0:T(8,128)(2,1)S(1)} %get-tuple-element.37), channel_id=1, source_target_pairs={{0,4},{1,5},{2,6},{3,7},{4,0},{5,1},{6,2},{7,3},{8,12},{9,13},{10,... | collective-permute-start | bytes 393224 | tf_op jit(solution)/shard_map/scatter_columns/ppermute | solution.py:307
  106.7 3.4 %collective-permute-start.7 = (bf16[256,256]{1,0:T(8,128)(2,1)S(1)}, bf16[256,256]{1,0:T(8,128)(2,1)S(1)}, u32[]{:S(2)}, u32[]{:S(2)}) collective-permute-start(bf16[256,256]{1,0:T(8,128)(2,1)S(1)} %get-tuple-element.38), channel_id=1, source_target_pairs={{0,2},{1,3},{2,4},{3,5},{4,6},{5,7},{6,0},{7,1},{8,10},{9,11},{10,... | collective-permute-start | bytes 393224 | tf_op jit(solution)/shard_map/scatter_columns/ppermute | solution.py:307
  110.1 2.5 %weight_grads.1 = (f32[96,2048]{1,0:T(8,128)}, f32[96,2048]{1,0:T(8,128)}, f32[96,2048]{1,0:T(8,128)}) custom-call(s32[3]{0:T(128)S(1)} %pad_add_fusion.where_ref, bf16[256,512]{1,0:T(8,128)(2,1)S(1)} %bitcast.22, bf16[256,512]{1,0:T(8,128)(2,1)S(1)} %collective-permute-done.refs_1_, bf16[256,512]{1,0:T(8,128)(2,1)S(1)} %collective-permute-done.1.refs_2_, ...), custom_call_target="tpu_custom_call" | custom-call | flops 301989888 | bytes 5242880 | tf_op jit(solution)/shard_map/weight_grads/pallas_call | solution.py:233
  112.6 5.5 %collective-permute-done.6 = bf16[256,256]{1,0:T(8,128)(2,1)S(1)} collective-permute-done((bf16[256,256]{1,0:T(8,128)(2,1)S(1)}, bf16[256,256]{1,0:T(8,128)(2,1)S(1)}, u32[]{:S(2)}, u32[]{:S(2)}) %collective-permute-start.6) | collective-permute-done | bytes 131104 | tf_op jit(solution)/shard_map/scatter_columns/ppermute | solution.py:307
  118.2 21.4 %all_to_all.20 = bf16[32,8,256]{2,1,0:T(8,128)(2,1)S(1)} all-to-all(bf16[32,8,256]{2,1,0:T(8,128)(2,1)S(1)} %fusion), channel_id=1, replica_groups=mesh['node'=32,'local'=32] {'node'}, dimensions={0} | all-to-all | bytes 262144 | tf_op jit(solution)/shard_map/rows_to_tokens/all_to_all | solution.py:252
  139.8 15.6 %all_to_all.21.in_ref = f32[32,2,384]{2,1,0:T(2,128)S(1)} all-to-all(f32[32,2,384]{2,1,0:T(2,128)S(1)} %rows_to_tokens.1), channel_id=1, replica_groups=mesh['node'=32,'local'=32] {'local'}, dimensions={0} | all-to-all | bytes 196608 | tf_op jit(solution)/shard_map/columns_to_tokens/all_to_all | solution.py:252
  (24 shorter events, 2.3 us)
Async XLA Ops:
  0.6 19.3 %copy-start.3 = (s32[64,8]{0,1:T(8,128)S(1)}, s32[64,8]{0,1:T(8,128)}, u32[]{:S(2)}) copy-start(s32[64,8]{0,1:T(8,128)} %param.10) | copy-start | bytes 6148
  0.6 19.3 %copy-start.4 = (s32[64,8]{0,1:T(8,128)S(1)}, s32[64,8]{0,1:T(8,128)}, u32[]{:S(2)}) copy-start(s32[64,8]{0,1:T(8,128)} %param.11) | copy-start | bytes 6148
  0.7 19.3 %copy-start.5 = (bf16[64,8]{0,1:T(8,128)(2,1)S(1)}, bf16[64,8]{0,1:T(8,128)(2,1)}, u32[]{:S(2)}) copy-start(bf16[64,8]{0,1:T(8,128)(2,1)} %param.12) | copy-start | bytes 3076
  2.0 41.6 %copy-start.2 = (bf16[1,96,2048]{2,1,0:T(8,128)(2,1)S(1)}, bf16[1,96,2048]{2,1,0:T(8,128)(2,1)}, u32[]{:S(2)}) copy-start(bf16[1,96,2048]{2,1,0:T(8,128)(2,1)} %param.15) | copy-start | bytes 1179652
  2.0 25.7 %all-to-all-start = ((bf16[32,2,512]{2,1,0:T(2,128)(2,1)}), bf16[32,2,512]{2,1,0:T(2,128)(2,1)S(1)}, u32[]{:S(2)}, u32[]{:S(2)}) async-start(bf16[32,2,512]{2,1,0:T(2,128)(2,1)} %tokens_to_columns.1), calls=%async_computation | async-start | bytes 131072 | tf_op jit(solution)/shard_map/tokens_to_columns/all_to_all | solution.py:252
  27.7 15.9 %copy-start = (bf16[1,96,2048]{2,1,0:T(8,128)(2,1)S(1)}, bf16[1,96,2048]{2,1,0:T(8,128)(2,1)}, u32[]{:S(2)}) copy-start(bf16[1,96,2048]{2,1,0:T(8,128)(2,1)} %param.13) | copy-start | bytes 1179652
  27.7 16.0 %copy-start.1 = (bf16[1,96,2048]{2,1,0:T(8,128)(2,1)S(1)}, bf16[1,96,2048]{2,1,0:T(8,128)(2,1)}, u32[]{:S(2)}) copy-start(bf16[1,96,2048]{2,1,0:T(8,128)(2,1)} %param.14) | copy-start | bytes 1179652
  28.7 35.0 %all-to-all-start.1 = ((bf16[32,8,512]{2,1,0:T(8,128)(2,1)}), bf16[32,8,512]{2,1,0:T(8,128)(2,1)S(1)}, u32[]{:S(2)}, u32[]{:S(2)}) async-start(bf16[32,8,512]{2,1,0:T(8,128)(2,1)} %bitcast.6), calls=%async_computation.1 | async-start | bytes 524288 | tf_op jit(solution)/shard_map/rows_to_experts/all_to_all | solution.py:252
  44.3 30.0 %collective-permute-start.3 = (bf16[288,1024]{1,0:T(8,128)(2,1)S(1)}, bf16[288,1024]{1,0:T(8,128)(2,1)S(1)}, u32[]{:S(2)}, u32[]{:S(2)}) collective-permute-start(bf16[288,1024]{1,0:T(8,128)(2,1)S(1)} %core_weights.2), channel_id=1, source_target_pairs={{0,1},{1,0},{2,3},{3,2},{4,5},{5,4},{6,7},{7,6},{8,9},{9,8},{10,11... | collective-permute-start | bytes 1769480 | tf_op jit(solution)/shard_map/core_weights/ppermute | solution.py:273
  63.7 11.4 %collective-permute-start.2 = (bf16[256,512]{1,0:T(8,128)(2,1)S(1)}, bf16[256,512]{1,0:T(8,128)(2,1)S(1)}, u32[]{:S(2)}, u32[]{:S(2)}) collective-permute-start(bf16[256,512]{1,0:T(8,128)(2,1)S(1)} %bitcast.17), channel_id=1, source_target_pairs={{0,6},{1,7},{2,0},{3,1},{4,2},{5,3},{6,4},{7,5},{8,14},{9,15},{10,... | collective-permute-start | bytes 786440 | tf_op jit(solution)/shard_map/gather_columns/ppermute | solution.py:285
  65.6 27.1 %collective-permute-start.1 = (bf16[256,512]{1,0:T(8,128)(2,1)S(1)}, bf16[256,512]{1,0:T(8,128)(2,1)S(1)}, u32[]{:S(2)}, u32[]{:S(2)}) collective-permute-start(bf16[256,512]{1,0:T(8,128)(2,1)S(1)} %bitcast.18), channel_id=1, source_target_pairs={{0,4},{1,5},{2,6},{3,7},{4,0},{5,1},{6,2},{7,3},{8,12},{9,13},{10,... | collective-permute-start | bytes 786440 | tf_op jit(solution)/shard_map/gather_columns/ppermute | solution.py:285
  72.4 20.2 %collective-permute-start = (bf16[256,512]{1,0:T(8,128)(2,1)S(1)}, bf16[256,512]{1,0:T(8,128)(2,1)S(1)}, u32[]{:S(2)}, u32[]{:S(2)}) collective-permute-start(bf16[256,512]{1,0:T(8,128)(2,1)S(1)} %bitcast.19), channel_id=1, source_target_pairs={{0,2},{1,3},{2,4},{3,5},{4,6},{5,7},{6,0},{7,1},{8,10},{9,11},{10,... | collective-permute-start | bytes 786440 | tf_op jit(solution)/shard_map/gather_columns/ppermute | solution.py:285
  93.8 5.5 %collective-permute-start.4 = (f32[256,640]{1,0:T(8,128)S(1)}, f32[256,640]{1,0:T(8,128)S(1)}, u32[]{:S(2)}, u32[]{:S(2)}) collective-permute-start(f32[256,640]{1,0:T(8,128)S(1)} %get-tuple-element.34.half_ref), channel_id=1, source_target_pairs={{0,1},{1,0},{2,3},{3,2},{4,5},{5,4},{6,7},{7,6},{8,9},{9,8},{10,11... | collective-permute-start | bytes 1966088 | tf_op jit(solution)/shard_map/hidden_grads/ppermute | solution.py:296
  100.6 9.5 %collective-permute-start.8 = (bf16[4,256,512]{2,1,0:T(8,128)(2,1)S(1)}, bf16[4,256,512]{2,1,0:T(8,128)(2,1)S(1)}, u32[]{:S(2)}, u32[]{:S(2)}) collective-permute-start(bf16[4,256,512]{2,1,0:T(8,128)(2,1)S(1)} %get-tuple-element.40), channel_id=1, source_target_pairs={{0,1},{1,0},{2,3},{3,2},{4,5},{5,4},{6,7},{7,6},{8,9},{9,8},{10,11... | collective-permute-start | bytes 3145736 | tf_op jit(solution)/shard_map/scatter_columns/ppermute | solution.py:310
  102.8 9.8 %collective-permute-start.5 = (bf16[256,256]{1,0:T(8,128)(2,1)S(1)}, bf16[256,256]{1,0:T(8,128)(2,1)S(1)}, u32[]{:S(2)}, u32[]{:S(2)}) collective-permute-start(bf16[256,256]{1,0:T(8,128)(2,1)S(1)} %get-tuple-element.36), channel_id=1, source_target_pairs={{0,6},{1,7},{2,0},{3,1},{4,2},{5,3},{6,4},{7,5},{8,14},{9,15},{10,... | collective-permute-start | bytes 393224 | tf_op jit(solution)/shard_map/scatter_columns/ppermute | solution.py:307
  104.8 13.4 %collective-permute-start.6 = (bf16[256,256]{1,0:T(8,128)(2,1)S(1)}, bf16[256,256]{1,0:T(8,128)(2,1)S(1)}, u32[]{:S(2)}, u32[]{:S(2)}) collective-permute-start(bf16[256,256]{1,0:T(8,128)(2,1)S(1)} %get-tuple-element.37), channel_id=1, source_target_pairs={{0,4},{1,5},{2,6},{3,7},{4,0},{5,1},{6,2},{7,3},{8,12},{9,13},{10,... | collective-permute-start | bytes 393224 | tf_op jit(solution)/shard_map/scatter_columns/ppermute | solution.py:307
  106.7 11.4 %collective-permute-start.7 = (bf16[256,256]{1,0:T(8,128)(2,1)S(1)}, bf16[256,256]{1,0:T(8,128)(2,1)S(1)}, u32[]{:S(2)}, u32[]{:S(2)}) collective-permute-start(bf16[256,256]{1,0:T(8,128)(2,1)S(1)} %get-tuple-element.38), channel_id=1, source_target_pairs={{0,2},{1,3},{2,4},{3,5},{4,6},{5,7},{6,0},{7,1},{8,10},{9,11},{10,... | collective-permute-start | bytes 393224 | tf_op jit(solution)/shard_map/scatter_columns/ppermute | solution.py:307
